TPU v7x, 32 devices: a whole 2x2x4 slice. The times are simulated.
32 devices in a mesh: row: 2 (over x), col: 4 (over z), fit: 4 (over y, core).
Axes of the slice: x: 2, y: 2, z: 4, core: 2. Of those that a mesh axis runs over, the one named last changes fastest.
Arguments:
- orbital_ints: bfloat16 [16, 40, 2560], P(('row', 'col'), None, 'fit'), may hold values from -0.83984375 to 0.83984375
- occ_energy: float32 [16], P(('row', 'col')), may hold values from -1.2 to -0.3
- pair_row: int32 [1024], P(('row', 'col')), may hold values from 0 to 7
- pair_col: int32 [1024], P(('row', 'col')), may hold values from 0 to 3
- virt_energy: float32 [40, 1024], P(None, ('row', 'col')), may hold values from 0.5 to 3
- amplitudes: float32 [40, 40, 1024], P(None, None, ('row', 'col')), may hold values from -1.8 to 1.8
- intersections: bfloat16 [40, 40, 16, 1024], P(None, None, 'fit', ('row', 'col')), may hold values from -1 to 1
- coupling_fock: float32 [16, 1024], P('fit', ('row', 'col')), may hold values from -0.25 to 0.25
- partner_owner: int32 [4, 1024, 4], P('fit', ('row', 'col')), may hold values from 0 to 7, all different within a row; in each aligned block of 128 rows (0 to 127, 128 to 255, ..., all dimensions but the last counted through in order) at most 128 rows name the same one
- partner_slot: int32 [4, 1024, 4], P('fit', ('row', 'col')), may hold values from 0 to 127
Outputs:
- new_amplitudes: float32 [40, 40, 1024], P(None, None, ('row', 'col'))
- residual: float32 [40, 40, 1024], P(None, None, ('row', 'col'))
Inputs may be any that keep to these rules, and one draw needn't show every extreme that they name: `partner_owner`: the 4 owners of one pair in one fit index differ; among the pairs of one group in one fit index (aligned blocks of 128 rows) no owner is named more than 128 times, a bound that some block reaches.
All inputs are finite; a program needn't handle non-finite values.
Results may differ from a plain program's by a relative error of at most 0.014.
Values may be sent and summed in bfloat16 or wider, within the bound.
A program may use at most 128 MiB of HBM per device.

v0:
```python
import math
import jax
import jax.numpy as jnp
from jax import lax
from jax.sharding import PartitionSpec as P

ITERS = 2


def on_device(
    orbital_ints,
    occ_energy,
    pair_row,
    pair_col,
    virt_energy,
    amplitudes,
    intersections,
    coupling_fock,
    partner_owner,
    partner_slot,
):
    row_count = lax.axis_size("row")
    col_count = lax.axis_size("col")
    group_count = row_count * col_count
    tile_size = amplitudes.shape[0]
    pair_count = amplitudes.shape[2]
    link_count = partner_owner.shape[2]
    capacity = 2 * pair_count * link_count // group_count
    row_ints, row_energy = (
        lax.all_gather(orbital_ints, "col", axis=0, tiled=True),
        lax.all_gather(occ_energy.astype(jnp.bfloat16), "col", axis=0, tiled=True).astype(
            occ_energy.dtype
        ),
    )
    col_ints, col_energy = (
        lax.all_gather(orbital_ints, "row", axis=0, tiled=True),
        lax.all_gather(occ_energy.astype(jnp.bfloat16), "row", axis=0, tiled=True).astype(
            occ_energy.dtype
        ),
    )
    block_width = math.gcd(pair_count, 128)
    blocks = pair_count // block_width

    def kernel_block(indices):
        first_ints = jnp.take(row_ints, indices[0], axis=0)
        second_ints = jnp.take(col_ints, indices[1], axis=0)
        return jnp.einsum(
            "pax,pbx->abp", first_ints, second_ints, preferred_element_type=jnp.float32
        )

    stacked = lax.map(
        kernel_block, (pair_row.reshape(blocks, block_width), pair_col.reshape(blocks, block_width))
    )
    partial_kernel = jnp.transpose(stacked, (1, 2, 0, 3)).reshape(tile_size, tile_size, pair_count)
    denominator = (
        virt_energy[:, None, :]
        + virt_energy[None, :, :]
        - (row_energy[pair_row] + col_energy[pair_col])[None, None, :]
    )
    owners = partner_owner[0].T.reshape(-1)
    owner_slots = partner_slot[0].T.reshape(-1)
    onehot = (owners[:, None] == jnp.arange(group_count, dtype=jnp.int32)[None, :]).astype(
        jnp.int32
    )
    position = jnp.sum((jnp.cumsum(onehot, axis=0) - 1) * onehot, axis=1)
    target = owners * capacity + position
    requests = jnp.zeros((group_count * capacity,), jnp.int32).at[target].set(owner_slots)
    incoming = lax.all_to_all(requests, ("row", "col"), split_axis=0, concat_axis=0, tiled=True)
    kernel = lax.psum(partial_kernel.astype(jnp.bfloat16), "fit").astype(jnp.float32)
    current = amplitudes
    residual = amplitudes
    for turn_index in range(ITERS):
        sent_tiles = current.astype(jnp.bfloat16)
        outgoing = jnp.take(sent_tiles, incoming, axis=2)
        returned = lax.all_to_all(outgoing, ("row", "col"), split_axis=2, concat_axis=2, tiled=True)
        coupled_tiles = jnp.take(returned, target, axis=2).reshape(
            tile_size, tile_size, link_count, pair_count
        )
        half_product = jnp.einsum(
            "abcp,bdcp->adcp", intersections, coupled_tiles, preferred_element_type=jnp.float32
        ).astype(jnp.bfloat16)
        coupled = jnp.einsum(
            "adcp,edcp->aecp", half_product, intersections, preferred_element_type=jnp.float32
        )
        coupling = jnp.sum(coupled * coupling_fock[None, None, :, :], axis=2)
        residual = (
            kernel
            + denominator * current
            - lax.psum(coupling.astype(jnp.bfloat16), "fit").astype(jnp.float32)
        )
        current = current - residual / denominator
    return (current, residual)


def solution(mesh):
    placed = (
        P(("row", "col"), None, "fit"),
        P(("row", "col")),
        P(("row", "col")),
        P(("row", "col")),
        P(None, ("row", "col")),
        P(None, None, ("row", "col")),
        P(None, None, "fit", ("row", "col")),
        P("fit", ("row", "col")),
        P("fit", ("row", "col"), None),
        P("fit", ("row", "col"), None),
    )
    return jax.shard_map(
        on_device,
        mesh=mesh,
        in_specs=placed,
        out_specs=(P(None, None, ("row", "col")), P(None, None, ("row", "col"))),
        check_vma=False,
    )
```

profile of v0, /device:TPU:0, one launch (start us, length us, event | category | flops | bytes accessed | tf_op | source)
XLA Modules:
  0.0 474.3 jit_solution(11859671098147663986)
XLA Ops:
  7.2 0.7 broadcast_multiply_fusion
  7.8 0.7 fusion.25
  8.5 1.1 reduce-window.6
  9.9 0.8 fusion.24
  10.7 3.2 scatter_custom_fusion
  13.9 7.3 %all-to-all-start = ((s32[8,128,1]{1,2,0:T(1,128)}), s32[8,128,1]{1,2,0:T(1,128)S(1)}, u32[]{:S(2)}, u32[]{:S(2)}) async-start(s32[8,128,1]{1,2,0:T(1,128)} %bitcast.29), calls=%async_computation | async-start | bytes 8192 | tf_op jit(solution)/shard_map/all_to_all | solution.py:68
  21.2 1.2 convert_element_type.66
  22.4 1.5 copy.61
  23.8 3.7 all-to-all-done
  27.6 11.1 %gather_fusion.2 = bf16[1024,40,40]{2,1,0:T(8,128)(2,1)} fusion(bf16[40,40,128]{1,0,2:T(8,128)(2,1)S(1)} %copy.61, s32[1024]{0:T(1024)S(1)} %fusion.26), kind=kCustom, calls=%fused_computation.clone | custom fusion | bytes 6557696 | tf_op jit(solution)/shard_map/jit(_take)/gather | solution.py:74
  38.7 11.5 %fusion.35 = bf16[1024,40,40]{2,1,0:T(8,128)(2,1)} fusion(bf16[1024,40,40]{2,1,0:T(8,128)(2,1)} %gather_fusion.2, pred[1024]{0:T(1024)(128)(4,1)S(1)} %compare_and_fusion), kind=kLoop, calls=%fused_computation.75 | loop fusion | flops 1638400 | bytes 6554624
  50.2 17.7 %reshape.213 = bf16[8,2,102400]{2,1,0:T(2,128)(2,1)} reshape(bf16[1024,40,40]{2,1,0:T(8,128)(2,1)} %fusion.35) | data formatting | bytes 6553600
  67.9 4.6 all-to-all-start.1
  72.6 0.6 dynamic-slice.3
  73.1 0.6 dynamic-slice.2
  75.1 0.2 dynamic-update-slice.1
  75.5 8.7 %all-reduce.1 = bf16[4]{0:T(256)(128)(2,1)S(1)} all-reduce(bf16[4]{0:T(256)(128)(2,1)S(1)} %dynamic-update-slice.1), channel_id=1, replica_groups=mesh['row'=2,'col'=4,'fit'=4] {'row'}, use_global_device_ids=true, to_apply=%add.1 | all-reduce | flops 4 | bytes 16
  84.2 48.3 %all-reduce = bf16[8]{0:T(256)(128)(2,1)S(1)} all-reduce(bf16[8]{0:T(256)(128)(2,1)S(1)} %dynamic-update-slice), channel_id=1, replica_groups=mesh['row'=2,'col'=4,'fit'=4] {'col'}, use_global_device_ids=true, to_apply=%add | all-reduce | flops 8 | bytes 32
  132.5 4.7 copy.63
  137.2 28.7 %all_gather.13 = bf16[8,40,640]{2,1,0:T(8,128)(2,1)S(1)} all-gather(bf16[2,40,640]{2,1,0:T(8,128)(2,1)S(1)} %copy-done.5), channel_id=1, replica_groups=mesh['row'=2,'col'=4,'fit'=4] {'col'}, dimensions={0}, use_global_device_ids=true | all-gather | bytes 512000 | tf_op jit(solution)/shard_map/all_gather | solution.py:30
  166.0 4.1 gather_fusion.1
  170.1 5.5 %all_gather.12 = bf16[4,40,640]{2,1,0:T(8,128)(2,1)S(1)} all-gather(bf16[2,40,640]{2,1,0:T(8,128)(2,1)S(1)} %copy-done.5), channel_id=1, replica_groups=mesh['row'=2,'col'=4,'fit'=4] {'row'}, dimensions={0}, use_global_device_ids=true | all-gather | bytes 307200 | tf_op jit(solution)/shard_map/all_gather | solution.py:36
  175.6 4.1 gather_fusion
  179.8 7.2 %fusion = bf16[128,40,40]{2,1,0:T(8,128)(2,1)S(1)} fusion(bf16[128,40,640]{2,1,0:T(8,128)(2,1)} %gather_fusion.1, bf16[128,40,640]{2,1,0:T(8,128)(2,1)} %gather_fusion, pred[128]{0:T(512)(128)(4,1)S(1)} %get-tuple-element.46, pred[128]{0:T(512)(128)(4,1)S(1)} %get-tuple-element.47), kind=kOutput, calls=%fused_computation.11 | convolution fusion | flops 268697600 | bytes 13517056 | tf_op jit(solution)/shard_map/while/body/eval_jaxpr/pax,pbx->abp/dot_general | solution.py:47
  187.0 1.9 copy.59
  188.9 18.7 %reshape.214 = bf16[1024,40,40]{2,1,0:T(8,128)(2,1)} reshape(bf16[8,2,102400]{2,1,0:T(2,128)(2,1)} %all-to-all-done.1) | data formatting | bytes 6553600
  207.6 7.9 %gather_fusion.3 = bf16[512,40,40]{2,1,0:T(8,128)(2,1)} fusion(bf16[40,40,1024]{1,0,2:T(8,128)(2,1)} %bitcast.87, s32[1024]{0:T(1024)S(1)} %pad_clamp_fusion), kind=kCustom, calls=%fused_computation.1.clone | custom fusion | bytes 3278848 | tf_op jit(solution)/shard_map/jit(_take)/gather | solution.py:76
  215.5 6.7 %broadcast_select_fusion.1 = bf16[512,40,40]{2,1,0:T(8,128)(2,1)} fusion(bf16[512,40,40]{2,1,0:T(8,128)(2,1)} %gather_fusion.3, pred[512]{0:T(512)(128)(4,1)S(1)} %get-tuple-element.32), kind=kLoop, calls=%fused_computation.23 | loop fusion | flops 819200 | bytes 3277312 | tf_op jit(solution)/shard_map/jit(_take)/select_n | solution.py:76
  222.2 9.7 %multiply_reduce_fusion.1 = bf16[128,40,40]{2,1,0:T(8,128)(2,1)S(1)} fusion(f32[4,128]{1,0:T(4,128)S(1)} %copy-done.10, bf16[40,40,4,128]{1,0,3,2:T(8,128)(2,1)} %copy.63, bf16[40,40,4,128]{1,0,3,2:T(8,128)(2,1)} %bitcast.89), kind=kOutput, calls=%fused_computation.10 | convolution fusion | flops 133324800 | bytes 3688448 | tf_op jit(solution)/shard_map/adcp,edcp->aecp/dot_general | solution.py:82
  231.8 1.7 copy.66
  233.6 0.3 all-reduce.6.cloned.1.call-start
  233.8 0.7 fusion.34
  234.5 0.7 fusion.33
  235.2 7.7 %fusion.29 = f32[128]{0:T(128)S(1)} fusion(f32[]{:T(128)} %bitcast.11, f32[]{:T(128)} %bitcast.12, f32[]{:T(128)} %bitcast.13, f32[]{:T(128)} %bitcast.14, f32[]{:T(128)} %bitcast.2, f32[]{:T(128)} %bitcast.3, f32[]{:T(128)} %bitcast.4, f32[]{:T(128)} %bitcast.5, f32[]{:T(128)} %bitcast.6, f32[]{:T(128)} %bitcast.7, f32[]{:T(128)} %bitcast.8, f32[]{:T(128)} %bitcast.9, ...), kind=kLoop, calls=%fused_computation.70 | loop fusion | flops 3456 | bytes 1584 | tf_op jit(solution)/shard_map/add | solution.py:58
  242.9 26.0 %all-reduce.8.cloned.1.call-done = (bf16[40,40,128]{2,1,0:T(8,128)(2,1)}, bf16[40,40,128]{2,1,0:T(8,128)(2,1)}) async-done(((bf16[40,40,128]{2,1,0:T(8,128)(2,1)}, bf16[40,40,128]{2,1,0:T(8,128)(2,1)}), (bf16[40,40,128]{2,1,0:T(8,128)(2,1)}, bf16[40,40,128]{2,1,0:T(8,128)(2,1)})) %all-reduce.8.cloned.1.call-update) | async-done | bytes 819216 | tf_op jit(solution)/shard_map/psum | solution.py:69
  268.9 1.4 fusion.31
  270.3 1.5 copy.67
  271.8 11.1 %gather_fusion.4 = bf16[1024,40,40]{2,1,0:T(8,128)(2,1)} fusion(bf16[40,40,128]{1,0,2:T(8,128)(2,1)S(1)} %copy.67, s32[1024]{0:T(1024)S(1)} %fusion.26), kind=kCustom, calls=%fused_computation.2.clone | custom fusion | bytes 6557696 | tf_op jit(solution)/shard_map/jit(_take)/gather | solution.py:74
  282.9 11.5 %fusion.36 = bf16[1024,40,40]{2,1,0:T(8,128)(2,1)} fusion(bf16[1024,40,40]{2,1,0:T(8,128)(2,1)} %gather_fusion.4, pred[1024]{0:T(1024)(128)(4,1)S(1)} %compare_and_fusion), kind=kLoop, calls=%fused_computation.76 | loop fusion | flops 1638400 | bytes 6554624
  294.4 16.9 %reshape.215 = bf16[8,2,102400]{2,1,0:T(2,128)(2,1)S(1)} reshape(bf16[1024,40,40]{2,1,0:T(8,128)(2,1)} %fusion.36) | data formatting | bytes 6553600
  311.3 78.9 %all_to_all.22 = bf16[8,2,102400]{2,1,0:T(2,128)(2,1)} all-to-all(bf16[8,2,102400]{2,1,0:T(2,128)(2,1)S(1)} %reshape.215), channel_id=1, replica_groups=mesh['row'=2,'col'=4,'fit'=4] {'row','col'}, dimensions={0} | all-to-all | bytes 6553600 | tf_op jit(solution)/shard_map/all_to_all | solution.py:75
  390.2 18.7 %reshape.216 = bf16[1024,40,40]{2,1,0:T(8,128)(2,1)} reshape(bf16[8,2,102400]{2,1,0:T(2,128)(2,1)} %all_to_all.22) | data formatting | bytes 6553600
  408.9 7.9 %gather_fusion.5 = bf16[512,40,40]{2,1,0:T(8,128)(2,1)} fusion(bf16[40,40,1024]{1,0,2:T(8,128)(2,1)} %bitcast.86, s32[1024]{0:T(1024)S(1)} %pad_clamp_fusion), kind=kCustom, calls=%fused_computation.3.clone | custom fusion | bytes 3278848 | tf_op jit(solution)/shard_map/jit(_take)/gather | solution.py:76
  416.8 6.7 %broadcast_select_fusion = bf16[512,40,40]{2,1,0:T(8,128)(2,1)} fusion(bf16[512,40,40]{2,1,0:T(8,128)(2,1)} %gather_fusion.5, pred[512]{0:T(512)(128)(4,1)S(1)} %get-tuple-element.32), kind=kLoop, calls=%fused_computation.22 | loop fusion | flops 819200 | bytes 3277312 | tf_op jit(solution)/shard_map/jit(_take)/select_n | solution.py:76
  423.5 9.7 %multiply_reduce_fusion = bf16[128,40,40]{2,1,0:T(8,128)(2,1)S(1)} fusion(f32[4,128]{1,0:T(4,128)S(1)} %copy-done.10, bf16[40,40,4,128]{1,0,3,2:T(8,128)(2,1)} %copy.63, bf16[40,40,4,128]{1,0,3,2:T(8,128)(2,1)} %bitcast.88), kind=kOutput, calls=%fused_computation.9 | convolution fusion | flops 133324800 | bytes 3688448 | tf_op jit(solution)/shard_map/adcp,edcp->aecp/dot_general | solution.py:82
  433.2 1.7 copy.72
  434.9 29.9 %all-reduce.6.cloned.1.call-done = bf16[40,40,128]{2,1,0:T(8,128)(2,1)} async-done(((bf16[40,40,128]{2,1,0:T(8,128)(2,1)}), bf16[40,40,128]{2,1,0:T(8,128)(2,1)}) %all-reduce.6.cloned.1.call-update) | async-done | bytes 409616 | tf_op jit(solution)/shard_map/psum | solution.py:89
  464.8 2.6 divide_subtract_fusion
  (49 shorter events, 0.7 us)
Async XLA Ops:
  13.9 13.7 %all-to-all-start = ((s32[8,128,1]{1,2,0:T(1,128)}), s32[8,128,1]{1,2,0:T(1,128)S(1)}, u32[]{:S(2)}, u32[]{:S(2)}) async-start(s32[8,128,1]{1,2,0:T(1,128)} %bitcast.29), calls=%async_computation | async-start | bytes 8192 | tf_op jit(solution)/shard_map/all_to_all | solution.py:68
  67.9 4.7 copy-start.13
  67.9 5.3 %copy-start.12 = (u32[32]{0:T(128)S(1)}, u32[32]{0:T(128)}, u32[]{:S(2)}) copy-start(u32[32]{0:T(128)} %constant.103) | copy-start | bytes 388
  67.9 7.2 %copy-start.11 = (f32[2]{0:T(128)S(1)}, f32[2]{0:T(128)}, u32[]{:S(2)}) copy-start(f32[2]{0:T(128)} %param.15) | copy-start | bytes 28
  67.9 64.6 %copy-start.2 = (bf16[40,40,4,128]{3,2,1,0:T(4,128)(2,1)S(1)}, bf16[40,40,4,128]{3,2,1,0:T(4,128)(2,1)}, u32[]{:S(2)}) copy-start(bf16[40,40,4,128]{3,2,1,0:T(4,128)(2,1)} %param.20) | copy-start | bytes 4915204
  67.9 69.4 %copy-start.9 = (s32[128]{0:T(128)S(1)}, s32[128]{0:T(128)}, u32[]{:S(2)}) copy-start(s32[128]{0:T(128)} %param.16) | copy-start | bytes 1540
  67.9 69.4 %copy-start.5 = (bf16[2,40,640]{2,1,0:T(8,128)(2,1)S(1)}, bf16[2,40,640]{2,1,0:T(8,128)(2,1)}, u32[]{:S(2)}) copy-start(bf16[2,40,640]{2,1,0:T(8,128)(2,1)} %param.14) | copy-start | bytes 307204
  67.9 121.0 %all-to-all-start.1 = ((bf16[8,2,102400]{2,1,0:T(2,128)(2,1)}), bf16[8,2,102400]{2,1,0:T(2,128)(2,1)}, u32[]{:S(2)}, u32[]{:S(2)}) async-start(bf16[8,2,102400]{2,1,0:T(2,128)(2,1)} %reshape.213), calls=%async_computation.1 | async-start | bytes 6553600 | tf_op jit(solution)/shard_map/all_to_all | solution.py:75
  72.5 196.4 %all-reduce.8.cloned.1.call-start = ((), (), s32[]{:S(2)}) async-start(), calls=%async_computation.4 | async-start | bytes 1638400 | tf_op jit(solution)/shard_map/psum | solution.py:69
  166.0 9.6 %copy-start.8 = (s32[128]{0:T(128)S(1)}, s32[128]{0:T(128)}, u32[]{:S(2)}) copy-start(s32[128]{0:T(128)} %param.17) | copy-start | bytes 1540
  179.7 9.1 %copy-start.7 = (s32[1,128,4]{1,2,0:T(4,128)S(1)}, s32[1,128,4]{1,2,0:T(4,128)}, u32[]{:S(2)}) copy-start(s32[1,128,4]{1,2,0:T(4,128)} %param.22) | copy-start | bytes 6148
  215.5 6.7 %copy-start.10 = (f32[4,128]{1,0:T(4,128)S(1)}, f32[4,128]{1,0:T(4,128)}, u32[]{:S(2)}) copy-start(f32[4,128]{1,0:T(4,128)} %param.21) | copy-start | bytes 6148
  222.2 46.8 %copy-start = (f32[40,40,128]{2,1,0:T(8,128)S(1)}, f32[40,40,128]{2,1,0:T(8,128)}, u32[]{:S(2)}) copy-start(f32[40,40,128]{2,1,0:T(8,128)} %param.19) | copy-start | bytes 2457604
  222.2 46.8 %copy-start.6 = (f32[40,128]{1,0:T(8,128)S(1)}, f32[40,128]{1,0:T(8,128)}, u32[]{:S(2)}) copy-start(f32[40,128]{1,0:T(8,128)} %param.18) | copy-start | bytes 61444
  233.6 231.3 %all-reduce.6.cloned.1.call-start = ((), (), s32[]{:S(2)}) async-start(), calls=%async_computation.3 | async-start | bytes 819200 | tf_op jit(solution)/shard_map/psum | solution.py:89
  423.5 41.4 %copy-start.1 = (f32[40,40,128]{2,1,0:T(8,128)S(1)}, f32[40,40,128]{2,1,0:T(8,128)}, u32[]{:S(2)}) copy-start(f32[40,40,128]{2,1,0:T(8,128)} %param.19) | copy-start | bytes 2457604
  423.5 41.4 %copy-start.3 = (bf16[40,40,128]{2,1,0:T(8,128)(2,1)S(1)}, bf16[40,40,128]{2,1,0:T(8,128)(2,1)}, u32[]{:S(2)}) copy-start(bf16[40,40,128]{2,1,0:T(8,128)(2,1)} %get-tuple-element.28) | copy-start | bytes 1228804
  423.5 41.4 %copy-start.4 = (bf16[40,40,128]{2,1,0:T(8,128)(2,1)S(1)}, bf16[40,40,128]{2,1,0:T(8,128)(2,1)}, u32[]{:S(2)}) copy-start(bf16[40,40,128]{2,1,0:T(8,128)(2,1)} %get-tuple-element.29) | copy-start | bytes 1228804
Sparse Core Ops, SparseCore 0:
  233.7 35.1 all-reduce.7
  435.0 29.7 all-reduce.5
where the time goes:
time: 475 us; the launch traced here: 474 us
  blocking collectives  170 us (36%)
  local copies, waits for them, and re-layouts  138 us (29%)
  waiting for transfers between devices  59.7 us (13%)
  other arithmetic  52.6 us (11%)
  matrix products  26.6 us (6%)
  between operations  15.5 us (3%)
  starting transfers between devices  12.2 us (3%)
    all_to_all x1, blocking collectives, on_device(): lax.all_to_all(outgoing, ('row', 'col'), split_axis=2, concat_axis=2, til...  78.9 us
    unnamed x39, local copies, waits for them, and re-layouts  78.5 us
    unnamed x2, blocking collectives  57 us
    psum x1, waiting for transfers between devices, on_device(): lax.psum(coupling.astype(jnp.bfloat16), 'fit').astype(jnp.float32)  29.9 us
    all_gather x1, blocking collectives, on_device(): lax.all_gather(orbital_ints, 'col', axis=0, tiled=True)  28.7 us
    psum x1, waiting for transfers between devices, on_device(): lax.psum(partial_kernel.astype(jnp.bfloat16), 'fit').astype(jnp.float32)  26 us
    unnamed x2, other arithmetic  22.9 us
    gather x2, local copies, waits for them, and re-layouts, on_device(): outgoing = jnp.take(sent_tiles, incoming, axis=2)  22.2 us
  transfers between devices with their start and end apart: 4, of which 3 were waited for; matrix products, arithmetic and copies ran while one was open for 7% of the time, Pallas kernels for 0%

commit v1 on v0

--- a/solution.py
+++ b/solution.py
@@ -5,6 +5,11 @@
 from jax.sharding import PartitionSpec as P
 
 ITERS = 2
+
+
+def add_all(x, mesh_axis):
+    parts = lax.all_gather(x, mesh_axis)
+    return jnp.sum(parts, axis=0)
 
 
 def on_device(
@@ -86,7 +91,7 @@
         residual = (
             kernel
             + denominator * current
-            - lax.psum(coupling.astype(jnp.bfloat16), "fit").astype(jnp.float32)
+            - add_all(coupling.astype(jnp.bfloat16), "fit").astype(jnp.float32)
         )
         current = current - residual / denominator
     return (current, residual)

time: 475 us -> 454 us (0.956)
  blocking collectives: 170 us -> 113 us
  waiting for transfers between devices: 59.7 us -> 93.1 us
    all_to_all x1, waiting for transfers between devices: 0.01 us -> 66.4 us  [on_device(): lax.all_to_all(outgoing, ('row', 'col'), split_axis=2, concat_axis=2, til...]
    unnamed x2, blocking collectives: 57 us -> 14.1 us
    psum x1 -> x0, waiting for transfers between devices: 29.9 us -> none  [on_device(): lax.psum(coupling.astype(jnp.bfloat16), 'fit').astype(jnp.float32)]
    psum x1, waiting for transfers between devices: 26 us -> 5.43 us  [on_device(): lax.psum(partial_kernel.astype(jnp.bfloat16), 'fit').astype(jnp.float32)]
    all_gather x0 -> x2, waiting for transfers between devices: none -> 17.5 us  [add_all(): parts = lax.all_gather(x, mesh_axis)]
    all_gather x1, blocking collectives: 28.7 us -> 14.3 us  [on_device(): lax.all_gather(orbital_ints, 'col', axis=0, tiled=True)]
  transfers between devices with their start and end apart: 4 -> 5, of which waited for: 3 -> 4; matrix products, arithmetic and copies ran while one was open for 7% -> 9% of each run, Pallas kernels for 0% -> 0%
where the time goes in v1:
time: 454 us; the launch traced here: 453 us
  local copies, waits for them, and re-layouts  138 us (30%)
  blocking collectives  113 us (25%)
  waiting for transfers between devices  93.1 us (21%)
  other arithmetic  54.8 us (12%)
  matrix products  26.7 us (6%)
  between operations  15.3 us (3%)
  starting transfers between devices  11.4 us (3%)
    unnamed x39, local copies, waits for them, and re-layouts  79.2 us
    all_to_all x1, blocking collectives, on_device(): lax.all_to_all(outgoing, ('row', 'col'), split_axis=2, concat_axis=2, til...  79 us
    all_to_all x1, waiting for transfers between devices, on_device(): lax.all_to_all(outgoing, ('row', 'col'), split_axis=2, concat_axis=2, til...  66.4 us
    unnamed x2, other arithmetic  22.8 us
    gather x2, local copies, waits for them, and re-layouts, on_device(): outgoing = jnp.take(sent_tiles, incoming, axis=2)  22.2 us
    dot_general x2, matrix products, on_device(): jnp.einsum('adcp,edcp->aecp', half_product, intersections, preferred_elem...  19.4 us
    all_gather x2, waiting for transfers between devices, add_all(): parts = lax.all_gather(x, mesh_axis)  17.5 us
    gather x2, local copies, waits for them, and re-layouts, on_device(): jnp.take(returned, target, axis=2)  15.8 us
  transfers between devices with their start and end apart: 5, of which 4 were waited for; matrix products, arithmetic and copies ran while one was open for 9% of the time, Pallas kernels for 0%

profile of v1, /device:TPU:0, one launch (start us, length us, event | category | flops | bytes accessed | tf_op | source)
XLA Modules:
  0.0 452.7 jit_solution(7398432759675700407)
XLA Ops:
  7.2 0.7 broadcast_multiply_fusion
  7.8 0.7 fusion.25
  8.5 1.1 reduce-window.6
  9.9 0.8 fusion.24
  10.7 3.2 scatter_custom_fusion
  13.9 7.3 %all-to-all-start = ((s32[8,128,1]{1,2,0:T(1,128)}), s32[8,128,1]{1,2,0:T(1,128)S(1)}, u32[]{:S(2)}, u32[]{:S(2)}) async-start(s32[8,128,1]{1,2,0:T(1,128)} %bitcast.29), calls=%async_computation | async-start | bytes 8192 | tf_op jit(solution)/shard_map/all_to_all | solution.py:73
  21.2 1.2 convert_element_type.90
  22.4 1.5 copy.95
  23.8 3.7 all-to-all-done
  27.6 11.1 %gather_fusion.2 = bf16[1024,40,40]{2,1,0:T(8,128)(2,1)} fusion(bf16[40,40,128]{1,0,2:T(8,128)(2,1)S(1)} %copy.95, s32[1024]{0:T(1024)S(1)} %fusion.26), kind=kCustom, calls=%fused_computation.clone | custom fusion | bytes 6557696 | tf_op jit(solution)/shard_map/jit(_take)/gather | solution.py:79
  38.7 11.4 %fusion.35 = bf16[1024,40,40]{2,1,0:T(8,128)(2,1)} fusion(bf16[1024,40,40]{2,1,0:T(8,128)(2,1)} %gather_fusion.2, pred[1024]{0:T(1024)(128)(4,1)S(1)} %compare_and_fusion), kind=kLoop, calls=%fused_computation.75 | loop fusion | flops 1638400 | bytes 6554624
  50.1 17.7 %reshape.231 = bf16[8,2,102400]{2,1,0:T(2,128)(2,1)} reshape(bf16[1024,40,40]{2,1,0:T(8,128)(2,1)} %fusion.35) | data formatting | bytes 6553600
  67.9 3.8 all-to-all-start.1
  71.9 6.5 %copy.97 = bf16[40,40,4,128]{1,0,3,2:T(8,128)(2,1)} copy(bf16[40,40,4,128]{3,2,1,0:T(4,128)(2,1)} %param.20) | data formatting | bytes 3276800 | tf_op args[6]
  78.4 66.4 %all-to-all-done.1 = bf16[8,2,102400]{2,1,0:T(2,128)(2,1)S(1)} async-done(((bf16[8,2,102400]{2,1,0:T(2,128)(2,1)}), bf16[8,2,102400]{2,1,0:T(2,128)(2,1)S(1)}, u32[]{:S(2)}, u32[]{:S(2)}) %all-to-all-start.1) | async-done | bytes 3276832 | tf_op jit(solution)/shard_map/all_to_all | solution.py:80
  144.8 17.6 %reshape.232 = bf16[1024,40,40]{2,1,0:T(8,128)(2,1)} reshape(bf16[8,2,102400]{2,1,0:T(2,128)(2,1)S(1)} %all-to-all-done.1) | data formatting | bytes 6553600
  162.4 7.9 %gather_fusion.3 = bf16[512,40,40]{2,1,0:T(8,128)(2,1)} fusion(bf16[40,40,1024]{1,0,2:T(8,128)(2,1)} %bitcast.89, s32[1024]{0:T(1024)S(1)} %pad_clamp_fusion), kind=kCustom, calls=%fused_computation.1.clone | custom fusion | bytes 3278848 | tf_op jit(solution)/shard_map/jit(_take)/gather | solution.py:81
  170.3 6.7 %broadcast_select_fusion.1 = bf16[512,40,40]{2,1,0:T(8,128)(2,1)} fusion(bf16[512,40,40]{2,1,0:T(8,128)(2,1)} %gather_fusion.3, pred[512]{0:T(512)(128)(4,1)S(1)} %get-tuple-element.34), kind=kLoop, calls=%fused_computation.23 | loop fusion | flops 819200 | bytes 3277312 | tf_op jit(solution)/shard_map/jit(_take)/select_n | solution.py:81
  177.1 9.7 %multiply_reduce_fusion.1 = bf16[128,40,40]{2,1,0:T(8,128)(2,1)S(1)} fusion(f32[4,128]{1,0:T(4,128)S(1)} %copy-done.10, bf16[40,40,4,128]{1,0,3,2:T(8,128)(2,1)} %copy.97, bf16[40,40,4,128]{1,0,3,2:T(8,128)(2,1)} %bitcast.91), kind=kOutput, calls=%fused_computation.10 | convolution fusion | flops 133324800 | bytes 3688448 | tf_op jit(solution)/shard_map/adcp,edcp->aecp/dot_general | solution.py:87
  186.7 1.7 copy.100
  189.1 0.6 dynamic-slice.2
  191.1 14.3 %all_gather.21 = bf16[8,40,640]{2,1,0:T(8,128)(2,1)S(1)} all-gather(bf16[2,40,640]{2,1,0:T(8,128)(2,1)S(1)} %copy-done.5), channel_id=1, replica_groups=mesh['row'=2,'col'=4,'fit'=4] {'col'}, dimensions={0}, use_global_device_ids=true | all-gather | bytes 512000 | tf_op jit(solution)/shard_map/all_gather | solution.py:35
  205.4 4.2 gather_fusion.1
  209.6 5.5 %all_gather.20 = bf16[4,40,640]{2,1,0:T(8,128)(2,1)S(1)} all-gather(bf16[2,40,640]{2,1,0:T(8,128)(2,1)S(1)} %copy-done.5), channel_id=1, replica_groups=mesh['row'=2,'col'=4,'fit'=4] {'row'}, dimensions={0}, use_global_device_ids=true | all-gather | bytes 307200 | tf_op jit(solution)/shard_map/all_gather | solution.py:41
  215.2 4.1 gather_fusion
  219.3 7.3 %fusion = bf16[128,40,40]{2,1,0:T(8,128)(2,1)S(1)} fusion(bf16[128,40,640]{2,1,0:T(8,128)(2,1)} %gather_fusion.1, bf16[128,40,640]{2,1,0:T(8,128)(2,1)} %gather_fusion, pred[128]{0:T(512)(128)(4,1)S(1)} %get-tuple-element.48, pred[128]{0:T(512)(128)(4,1)S(1)} %get-tuple-element.49), kind=kOutput, calls=%fused_computation.11 | convolution fusion | flops 268697600 | bytes 13517056 | tf_op jit(solution)/shard_map/while/body/eval_jaxpr/pax,pbx->abp/dot_general | solution.py:52
  226.6 1.9 copy.93
  228.9 4.9 %all-reduce.1 = bf16[4]{0:T(256)(128)(2,1)S(1)} all-reduce(bf16[4]{0:T(256)(128)(2,1)S(1)} %dynamic-update-slice.1), channel_id=1, replica_groups=mesh['row'=2,'col'=4,'fit'=4] {'row'}, use_global_device_ids=true, to_apply=%add.1 | all-reduce | flops 4 | bytes 16
  233.8 9.1 %all-reduce = bf16[8]{0:T(256)(128)(2,1)S(1)} all-reduce(bf16[8]{0:T(256)(128)(2,1)S(1)} %dynamic-update-slice), channel_id=1, replica_groups=mesh['row'=2,'col'=4,'fit'=4] {'col'}, use_global_device_ids=true, to_apply=%add | all-reduce | flops 8 | bytes 32
  243.0 0.7 fusion.34
  243.6 0.7 fusion.33
  244.3 7.6 %fusion.29 = f32[128]{0:T(128)S(1)} fusion(f32[]{:T(128)} %bitcast.11, f32[]{:T(128)} %bitcast.12, f32[]{:T(128)} %bitcast.13, f32[]{:T(128)} %bitcast.14, f32[]{:T(128)} %bitcast.2, f32[]{:T(128)} %bitcast.3, f32[]{:T(128)} %bitcast.4, f32[]{:T(128)} %bitcast.5, f32[]{:T(128)} %bitcast.6, f32[]{:T(128)} %bitcast.7, f32[]{:T(128)} %bitcast.8, f32[]{:T(128)} %bitcast.9, ...), kind=kLoop, calls=%fused_computation.70 | loop fusion | flops 3456 | bytes 1584 | tf_op jit(solution)/shard_map/add | solution.py:63
  251.9 1.8 reduce_sum.56
  253.8 5.4 %all-reduce.4.cloned.1.call-done = bf16[40,40,128]{2,1,0:T(8,128)(2,1)} async-done(((bf16[40,40,128]{2,1,0:T(8,128)(2,1)}), bf16[40,40,128]{2,1,0:T(8,128)(2,1)}) %all-reduce.4.cloned.1.call-update) | async-done | bytes 409616 | tf_op jit(solution)/shard_map/psum | solution.py:74
  259.2 1.3 fusion.31
  260.5 1.5 copy.101
  262.0 11.1 %gather_fusion.4 = bf16[1024,40,40]{2,1,0:T(8,128)(2,1)} fusion(bf16[40,40,128]{1,0,2:T(8,128)(2,1)S(1)} %copy.101, s32[1024]{0:T(1024)S(1)} %fusion.26), kind=kCustom, calls=%fused_computation.2.clone | custom fusion | bytes 6557696 | tf_op jit(solution)/shard_map/jit(_take)/gather | solution.py:79
  273.1 11.4 %fusion.36 = bf16[1024,40,40]{2,1,0:T(8,128)(2,1)} fusion(bf16[1024,40,40]{2,1,0:T(8,128)(2,1)} %gather_fusion.4, pred[1024]{0:T(1024)(128)(4,1)S(1)} %compare_and_fusion), kind=kLoop, calls=%fused_computation.76 | loop fusion | flops 1638400 | bytes 6554624
  284.5 16.9 %reshape.233 = bf16[8,2,102400]{2,1,0:T(2,128)(2,1)S(1)} reshape(bf16[1024,40,40]{2,1,0:T(8,128)(2,1)} %fusion.36) | data formatting | bytes 6553600
  301.4 79.0 %all_to_all.22 = bf16[8,2,102400]{2,1,0:T(2,128)(2,1)} all-to-all(bf16[8,2,102400]{2,1,0:T(2,128)(2,1)S(1)} %reshape.233), channel_id=1, replica_groups=mesh['row'=2,'col'=4,'fit'=4] {'row','col'}, dimensions={0} | all-to-all | bytes 6553600 | tf_op jit(solution)/shard_map/all_to_all | solution.py:80
  380.5 18.7 %reshape.234 = bf16[1024,40,40]{2,1,0:T(8,128)(2,1)} reshape(bf16[8,2,102400]{2,1,0:T(2,128)(2,1)} %all_to_all.22) | data formatting | bytes 6553600
  399.2 7.9 %gather_fusion.5 = bf16[512,40,40]{2,1,0:T(8,128)(2,1)} fusion(bf16[40,40,1024]{1,0,2:T(8,128)(2,1)} %bitcast.88, s32[1024]{0:T(1024)S(1)} %pad_clamp_fusion), kind=kCustom, calls=%fused_computation.3.clone | custom fusion | bytes 3278848 | tf_op jit(solution)/shard_map/jit(_take)/gather | solution.py:81
  407.1 6.6 %broadcast_select_fusion = bf16[512,40,40]{2,1,0:T(8,128)(2,1)} fusion(bf16[512,40,40]{2,1,0:T(8,128)(2,1)} %gather_fusion.5, pred[512]{0:T(512)(128)(4,1)S(1)} %get-tuple-element.34), kind=kLoop, calls=%fused_computation.22 | loop fusion | flops 819200 | bytes 3277312 | tf_op jit(solution)/shard_map/jit(_take)/select_n | solution.py:81
  413.7 9.7 %multiply_reduce_fusion = bf16[128,40,40]{2,1,0:T(8,128)(2,1)S(1)} fusion(f32[4,128]{1,0:T(4,128)S(1)} %copy-done.10, bf16[40,40,4,128]{1,0,3,2:T(8,128)(2,1)} %copy.97, bf16[40,40,4,128]{1,0,3,2:T(8,128)(2,1)} %bitcast.90), kind=kOutput, calls=%fused_computation.9 | convolution fusion | flops 133324800 | bytes 3688448 | tf_op jit(solution)/shard_map/adcp,edcp->aecp/dot_general | solution.py:87
  423.5 1.7 copy.106
  425.2 17.4 %all-gather.7.cloned.1.call-done = bf16[160,40,128]{2,1,0:T(8,128)(2,1)} async-done(((bf16[40,40,128]{2,1,0:T(8,128)(2,1)}), bf16[160,40,128]{2,1,0:T(8,128)(2,1)}) %all-gather.7.cloned.1.call-update) | async-done | bytes 1638416 | tf_op jit(solution)/shard_map/all_gather | solution.py:11
  442.7 1.8 reduce_sum.58
  444.6 1.6 divide_subtract_fusion
  (54 shorter events, 1.8 us)
Async XLA Ops:
  13.9 13.7 %all-to-all-start = ((s32[8,128,1]{1,2,0:T(1,128)}), s32[8,128,1]{1,2,0:T(1,128)S(1)}, u32[]{:S(2)}, u32[]{:S(2)}) async-start(s32[8,128,1]{1,2,0:T(1,128)} %bitcast.29), calls=%async_computation | async-start | bytes 8192 | tf_op jit(solution)/shard_map/all_to_all | solution.py:73
  67.9 10.5 %copy-start.7 = (s32[1,128,4]{1,2,0:T(4,128)S(1)}, s32[1,128,4]{1,2,0:T(4,128)}, u32[]{:S(2)}) copy-start(s32[1,128,4]{1,2,0:T(4,128)} %param.22) | copy-start | bytes 6148
  67.9 77.0 %all-to-all-start.1 = ((bf16[8,2,102400]{2,1,0:T(2,128)(2,1)}), bf16[8,2,102400]{2,1,0:T(2,128)(2,1)S(1)}, u32[]{:S(2)}, u32[]{:S(2)}) async-start(bf16[8,2,102400]{2,1,0:T(2,128)(2,1)} %reshape.231), calls=%async_computation.1 | async-start | bytes 6553600 | tf_op jit(solution)/shard_map/all_to_all | solution.py:80
  71.7 180.3 %all-gather.5.cloned.1.call-start = ((), (), s32[]{:S(2)}) async-start(), calls=%async_computation.4 | async-start | bytes 2048000 | tf_op jit(solution)/shard_map/all_gather | solution.py:11
  170.3 6.7 %copy-start.10 = (f32[4,128]{1,0:T(4,128)S(1)}, f32[4,128]{1,0:T(4,128)}, u32[]{:S(2)}) copy-start(f32[4,128]{1,0:T(4,128)} %param.21) | copy-start | bytes 6148
  177.0 11.5 %copy-start.13 = (u32[32]{0:T(128)S(1)}, u32[32]{0:T(128)}, u32[]{:S(2)}) copy-start(u32[32]{0:T(128)} %constant.111) | copy-start | bytes 388
  177.0 12.1 %copy-start.12 = (u32[32]{0:T(128)S(1)}, u32[32]{0:T(128)}, u32[]{:S(2)}) copy-start(u32[32]{0:T(128)} %constant.106) | copy-start | bytes 388
  177.0 14.0 %copy-start.11 = (f32[2]{0:T(128)S(1)}, f32[2]{0:T(128)}, u32[]{:S(2)}) copy-start(f32[2]{0:T(128)} %param.15) | copy-start | bytes 28
  177.0 14.0 %copy-start.9 = (s32[128]{0:T(128)S(1)}, s32[128]{0:T(128)}, u32[]{:S(2)}) copy-start(s32[128]{0:T(128)} %param.16) | copy-start | bytes 1540
  177.1 14.0 %copy-start.5 = (bf16[2,40,640]{2,1,0:T(8,128)(2,1)S(1)}, bf16[2,40,640]{2,1,0:T(8,128)(2,1)}, u32[]{:S(2)}) copy-start(bf16[2,40,640]{2,1,0:T(8,128)(2,1)} %param.14) | copy-start | bytes 307204
  188.5 70.7 %all-reduce.4.cloned.1.call-start = ((), (), s32[]{:S(2)}) async-start(), calls=%async_computation.3 | async-start | bytes 819200 | tf_op jit(solution)/shard_map/psum | solution.py:74
  205.4 9.8 %copy-start.8 = (s32[128]{0:T(128)S(1)}, s32[128]{0:T(128)}, u32[]{:S(2)}) copy-start(s32[128]{0:T(128)} %param.17) | copy-start | bytes 1540
  219.2 40.0 %copy-start = (f32[40,40,128]{2,1,0:T(8,128)S(1)}, f32[40,40,128]{2,1,0:T(8,128)}, u32[]{:S(2)}) copy-start(f32[40,40,128]{2,1,0:T(8,128)} %param.19) | copy-start | bytes 2457604
  219.2 40.0 %copy-start.6 = (f32[40,128]{1,0:T(8,128)S(1)}, f32[40,128]{1,0:T(8,128)}, u32[]{:S(2)}) copy-start(f32[40,128]{1,0:T(8,128)} %param.18) | copy-start | bytes 61444
  228.9 213.8 %all-gather.7.cloned.1.call-start = ((), (), s32[]{:S(2)}) async-start(), calls=%async_computation.5 | async-start | bytes 2048000 | tf_op jit(solution)/shard_map/all_gather | solution.py:11
  253.8 5.4 %copy-start.2 = (bf16[40,40,128]{2,1,0:T(8,128)(2,1)}, bf16[40,40,128]{2,1,0:T(8,128)(2,1)S(1)}, u32[]{:S(2)}) copy-start(bf16[40,40,128]{2,1,0:T(8,128)(2,1)S(1)} %reduce_sum.56) | copy-start | bytes 1228804
  413.7 30.8 %copy-start.1 = (f32[40,40,128]{2,1,0:T(8,128)S(1)}, f32[40,40,128]{2,1,0:T(8,128)}, u32[]{:S(2)}) copy-start(f32[40,40,128]{2,1,0:T(8,128)} %param.19) | copy-start | bytes 2457604
  413.7 30.8 %copy-start.3 = (bf16[40,40,128]{2,1,0:T(8,128)(2,1)S(1)}, bf16[40,40,128]{2,1,0:T(8,128)(2,1)}, u32[]{:S(2)}) copy-start(bf16[40,40,128]{2,1,0:T(8,128)(2,1)} %copy-done.2) | copy-start | bytes 1228804
  413.7 30.8 %copy-start.4 = (bf16[40,40,128]{2,1,0:T(8,128)(2,1)S(1)}, bf16[40,40,128]{2,1,0:T(8,128)(2,1)}, u32[]{:S(2)}) copy-start(bf16[40,40,128]{2,1,0:T(8,128)(2,1)} %all-reduce.4.cloned.1.call-done) | copy-start | bytes 1228804
Sparse Core Ops, SparseCore 0:
  188.6 17.3 all-gather.4
  229.0 30.1 all-reduce.3
  425.3 17.2 all-gather.6
